TPU v7x, 32 devices: a whole 2x2x4 slice. The times are simulated.
32 devices in a mesh: slab: 8 (over y, x, core), term: 4 (over z).
Axes of the slice: x: 2, y: 2, z: 4, core: 2. Of those that a mesh axis runs over, the one named last changes fastest.
Arguments:
- panels: float32 [64, 1024], P(None, 'term'), may hold values from -0.1875 to 0.1875
- block_phase: int32 [2, 64], P(None, 'term'), may hold values from 0 to 4194303
- target_owner: int32 [16384, 1], P(('slab', 'term')), may hold values from 0 to 31; in each aligned block of 512 rows (0 to 511, 512 to 1023, ...) at most 32 rows name the same one
- target_cell: int32 [16384], P(('slab', 'term')), may hold values from 0 to 6143
- target_offset: int32 [16384], P(('slab', 'term')), may hold values from 0 to 255
Outputs:
- grid_values: float32 [64, 196608], P(None, ('slab', 'term'))
- target_values: float32 [64, 16384], P(None, ('slab', 'term'))
Inputs may be any that keep to these rules, and one draw needn't show every extreme that they name: `target_owner`: among the 512 targets of one device no owner appears more than 32 times, and some owner appears exactly 32 times.
All inputs are finite; a program needn't handle non-finite values.
Results may differ from a plain program's by a relative error of at most 0.0003.
Values sent between devices are 32-bit elements; how exact they have to be, the bound alone decides.
A program may use at most 256 MiB of HBM per device.

v0:
```python
import math

import jax
import jax.numpy as jnp
from jax import lax
from jax.sharding import PartitionSpec as P

TAPS = 256
OFFQ = 256
ROOTQ = 2048
GS = 6144
PHASEQ = 4194304


def extended_2(x, sides, width):
    for axis, dim in sides:
        devices, length = (lax.axis_size(axis), x.shape[dim])
        up = [(i, (i + 1) % devices) for i in range(devices - 1)]
        down = [(j, i) for i, j in up]
        last = lax.slice_in_dim(x, length - width, length, axis=dim)
        first = lax.slice_in_dim(x, 0, width, axis=dim)
        before = lax.ppermute(last, axis, up)
        after = lax.ppermute(first, axis, down)
        x = jnp.concatenate([before, x, after], axis=dim)
    return x


def chebyshev(xpos, order):
    rows = [jnp.ones_like(xpos), xpos]
    for j in range(2, order):
        rows.append(2.0 * xpos * rows[-1] - rows[-2])
    return jnp.stack(rows[:order], 0)


def block_turns(phases, gpos):
    wrapped = gpos % PHASEQ
    g_high = wrapped // ROOTQ
    g_low = wrapped % ROOTQ
    p_high = phases[1] // ROOTQ
    p_low = phases[1] % ROOTQ
    cross = (g_high[None, :] * p_low[:, None] + g_low[None, :] * p_high[:, None]) % ROOTQ
    total = phases[0][:, None] + cross * ROOTQ + g_low[None, :] * p_low[:, None]
    return (total % PHASEQ).astype(jnp.int32)


def grid_terms(coeffs, phases, gpos):
    nblk = phases.shape[1]
    order = coeffs.shape[1] // nblk
    half = coeffs.shape[0] // 2
    width = gpos.shape[0]
    local = gpos - gpos // GS * GS
    xpos = (2 * local + 1).astype(jnp.float32) / GS - 1.0
    cheb = chebyshev(xpos, order)
    turns = block_turns(phases, gpos)
    angle = turns.astype(jnp.float32) * (2.0 * math.pi / PHASEQ)
    basis_cos = (jnp.cos(angle)[:, None, :] * cheb[None, :, :]).reshape(nblk * order, width)
    basis_sin = (jnp.sin(angle)[:, None, :] * cheb[None, :, :]).reshape(nblk * order, width)
    with_cos = jnp.dot(
        coeffs, basis_cos, precision=lax.Precision.HIGHEST, preferred_element_type=jnp.float32
    )
    with_sin = jnp.dot(
        coeffs, basis_sin, precision=lax.Precision.HIGHEST, preferred_element_type=jnp.float32
    )
    real_part = with_cos[:half] - with_sin[half:]
    imag_part = with_sin[:half] + with_cos[half:]
    return jnp.concatenate([real_part, imag_part], 0)


def kernel_matrix(cell_ids, offset_ids, valid, width):
    frac = (offset_ids.astype(jnp.float32) + 0.5) / OFFQ
    column = jnp.arange(width, dtype=jnp.int32)
    place = column[None, :] - cell_ids[:, None] - 1
    inside = (place >= 0) & (place < TAPS) & valid[:, None]
    dist = (place - TAPS // 2 + 1).astype(jnp.float32) - frac[:, None]
    parity = jnp.where(place % 2 == 0, 1.0, -1.0).astype(jnp.float32)
    weights = (
        parity
        * jnp.sin(math.pi * frac)[:, None]
        / (math.pi * dist)
        * jnp.exp(-18.0 * dist * dist / (TAPS * TAPS))
    )
    return jnp.where(inside, weights, 0.0)


def body(panels, block_phase, target_owner, target_cell, target_offset):
    n_slab = lax.axis_size("slab")
    n_term = lax.axis_size("term")
    n_dev = n_slab * n_term
    device = lax.axis_index("slab") * n_term + lax.axis_index("term")
    rim = TAPS // 2
    channels = panels.shape[0]
    tgt_count = target_cell.shape[0]
    capacity = max(2, 2 * tgt_count // n_dev)
    gpos = device * GS + jnp.arange(GS, dtype=jnp.int32)
    grid = grid_terms(
        lax.all_gather(panels, "term", axis=1, tiled=True),
        lax.all_gather(block_phase, "term", axis=1, tiled=True),
        gpos,
    )
    extended = extended_2(grid, ((("slab", "term"), 1),), rim)
    owners = target_owner[:, 0]
    one_hot = (owners[:, None] == jnp.arange(n_dev, dtype=jnp.int32)[None, :]).astype(jnp.bfloat16)
    order_idx = jnp.arange(tgt_count, dtype=jnp.int32)
    earlier = (order_idx[:, None] > order_idx[None, :]).astype(jnp.bfloat16)
    before = jnp.dot(earlier, one_hot, preferred_element_type=jnp.float32)
    rank = jnp.sum(before * one_hot.astype(jnp.float32), axis=1).astype(jnp.int32)
    slot = owners * capacity + rank
    codes = (
        jnp.full((n_dev * capacity,), -1, jnp.int32)
        .at[slot]
        .set(target_cell * OFFQ + target_offset)
    )
    codes = codes.reshape(n_slab, n_term, capacity)
    arrived = lax.all_to_all(
        lax.all_to_all(codes, "slab", split_axis=0, concat_axis=0, tiled=True),
        "term",
        split_axis=1,
        concat_axis=1,
        tiled=True,
    )
    arrived = arrived.reshape(-1)
    slots = arrived.shape[0]
    valid = arrived >= 0
    cells = jnp.where(valid, arrived // OFFQ, 0)
    offsets = jnp.where(valid, arrived % OFFQ, 0)
    width = extended.shape[1]
    group = 512
    parts_out = []
    for begin in range(0, slots, group):
        kernel = kernel_matrix(
            cells[begin : begin + group],
            offsets[begin : begin + group],
            valid[begin : begin + group],
            width,
        )
        parts_out.append(
            lax.dot_general(
                extended,
                kernel,
                (((1,), (1,)), ((), ())),
                precision=lax.Precision.HIGHEST,
                preferred_element_type=jnp.float32,
            )
        )
    values = jnp.concatenate(parts_out, 1)
    outgoing = values.reshape(channels, n_slab, n_term, capacity)
    returned = lax.all_to_all(
        lax.all_to_all(outgoing, "slab", split_axis=1, concat_axis=1, tiled=True),
        "term",
        split_axis=2,
        concat_axis=2,
        tiled=True,
    )
    table = returned.reshape(channels, n_dev * capacity)
    return (grid, jnp.take(table, slot, axis=1))


def solution(mesh):
    placed = (
        P(None, "term"),
        P(None, "term"),
        P(("slab", "term"), None),
        P(("slab", "term")),
        P(("slab", "term")),
    )
    return jax.shard_map(
        body,
        mesh=mesh,
        in_specs=placed,
        out_specs=(P(None, ("slab", "term")), P(None, ("slab", "term"))),
        check_vma=False,
    )
```

profile of v0, /device:TPU:0, one launch (start us, length us, event | category | flops | bytes accessed | tf_op | source)
XLA Modules:
  0.0 212.3 jit_solution(2482263377597709517)
XLA Ops:
  0.6 1.0 fusion.89
  1.7 1.2 and_reduce_fusion
  2.9 0.0 copy-start
  2.9 0.7 multiply_add_fusion.2
  3.6 0.0 copy-done
  3.6 2.4 %scatter_custom_fusion = s32[1024]{0:T(1024)S(1)} fusion(s32[512]{0:T(512)S(1)} %bitcast.55, s32[512]{0:T(512)S(1)} %multiply_add_fusion.2, s32[]{:T(128)} %constant.181.clone.1), kind=kCustom, calls=%fused_computation.176 | custom fusion | bytes 4100 | tf_op jit(solution)/shard_map/scatter | solution.py:111
  6.1 0.1 reshape.481
  6.1 0.7 reshape.506
  6.8 5.2 %all-to-all-start = ((s32[8,1,128]{2,1,0:T(1,128)}), s32[8,1,128]{2,1,0:T(1,128)}, u32[]{:S(2)}, u32[]{:S(2)}) async-start(s32[8,1,128]{2,1,0:T(1,128)} %reshape.506), calls=%async_computation | async-start | bytes 8192 | tf_op jit(solution)/shard_map/all_to_all | solution.py:115
  12.0 0.4 multiply_subtract_fusion
  12.4 0.4 multiply_subtract_fusion.2
  12.7 1.0 multiply_subtract_fusion.4
  13.7 0.9 multiply_subtract_fusion.6
  14.6 0.9 multiply_subtract_fusion.8
  15.5 0.9 multiply_subtract_fusion.10
  16.4 0.8 multiply_subtract_fusion.12
  17.2 0.8 multiply_add_fusion.1
  18.1 11.5 %all-gather = s32[4,16,2]{1,2,0:T(2,128)S(1)} all-gather(s32[1,16,2]{1,2,0:T(2,128)} %bitcast.59), channel_id=1, replica_groups=mesh['slab'=8,'term'=4] {'term'}, dimensions={0}, use_global_device_ids=true | all-gather | bytes 640 | tf_op jit(solution)/shard_map/all_gather | solution.py:97
  29.6 0.1 reshape.502
  29.7 14.4 %all_gather.7 = f32[64,1024]{1,0:T(8,128)S(1)} all-gather(f32[64,256]{1,0:T(8,128)} %param.5), channel_id=1, replica_groups=mesh['slab'=8,'term'=4] {'term'}, dimensions={1}, use_global_device_ids=true | all-gather | bytes 327680 | tf_op jit(solution)/shard_map/all_gather | solution.py:96
  44.1 7.0 %fusion.90 = (f32[64,6144]{1,0:T(8,128)S(1)}, f32[64,6144]{1,0:T(8,128)S(1)}) fusion(s32[64]{0:T(128)S(1)} %and_select_fusion.1, s32[6144]{0:T(1024)S(1)} %get-tuple-element.32, s32[64]{0:T(128)S(1)} %get-tuple-element.12, s32[6144]{0:T(1024)S(1)} %get-tuple-element.33, s32[64]{0:T(128)S(1)} %slice_bitcast_fusion), kind=kLoop, calls=%fused_computation.116 | loop fusion | flops 12189696 | bytes 3195648 | tf_op jit(solution)/shard_map/sin | solution.py:57
  51.1 3.5 %stack.2 = f32[16,6144]{1,0:T(8,128)} concatenate(f32[1,6144]{1,0:T(1,128)S(1)} %stack_broadcast_in_dim.3, f32[1,6144]{1,0:T(1,128)} %multiply_add_fusion.1, f32[1,6144]{1,0:T(1,128)} %get-tuple-element.47, f32[1,6144]{1,0:T(1,128)} %get-tuple-element.46, f32[1,6144]{1,0:T(1,128)} %get-tuple-element.45, f32[1,6144]{1,0:T(1,128)} %get-tuple-element.44, ...), dimensions={0} | concatenate | bytes 786432 | tf_op jit(solution)/shard_map/stack | solution.py:32
  54.6 18.4 %broadcast_multiply_fusion = (f32[64,16,6144]{2,1,0:T(8,128)}, f32[64,16,6144]{2,1,0:T(8,128)}) fusion(f32[64,6144]{1,0:T(8,128)S(1)} %get-tuple-element.20, f32[16,6144]{1,0:T(8,128)} %stack.2, f32[64,6144]{1,0:T(8,128)S(1)} %get-tuple-element.21), kind=kLoop, calls=%fused_computation.56 | loop fusion | flops 12582912 | bytes 53870592 | tf_op jit(solution)/shard_map/mul | solution.py:57
  73.1 19.5 %convolution_bitcast_fusion = f32[64,6144]{1,0:T(8,128)S(1)} fusion(f32[1024,6144]{1,0:T(8,128)} %bitcast.49, f32[64,1024]{1,0:T(8,128)S(1)} %all_gather.7), kind=kOutput, calls=%fused_computation.58 | convolution fusion | flops 4831838208 | bytes 27000832 | tf_op jit(solution)/shard_map/dot_general | solution.py:61
  92.6 19.5 %convolution_bitcast_fusion.1 = f32[64,6144]{1,0:T(8,128)S(1)} fusion(f32[1024,6144]{1,0:T(8,128)} %bitcast.48, f32[64,1024]{1,0:T(8,128)S(1)} %all_gather.7), kind=kOutput, calls=%fused_computation.59 | convolution fusion | flops 4831838208 | bytes 27000832 | tf_op jit(solution)/shard_map/dot_general | solution.py:58
  112.1 0.2 slice_subtract_fusion
  112.3 0.0 all-to-all-done
  112.3 0.5 broadcast.1601
  112.8 1.3 reduce.2
  114.2 0.1 reshape.507
  114.3 0.7 reshape.508
  114.9 3.2 %all-to-all-start.1 = ((s32[4,1,256]{2,1,0:T(1,128)}), s32[4,1,256]{2,1,0:T(1,128)S(1)}, u32[]{:S(2)}, u32[]{:S(2)}) async-start(s32[4,1,256]{2,1,0:T(1,128)} %reshape.508), calls=%async_computation.1 | async-start | bytes 8192 | tf_op jit(solution)/shard_map/all_to_all | solution.py:114
  118.2 3.9 %collective-permute-start = (f32[64,128]{1,0:T(8,128)S(1)}, f32[64,128]{1,0:T(8,128)S(1)}, u32[]{:S(2)}, u32[]{:S(2)}) collective-permute-start(f32[64,128]{1,0:T(8,128)S(1)} %get-tuple-element.16), channel_id=1, source_target_pairs={{0,1},{1,2},{2,3},{3,4},{4,5},{5,6},{6,7},{7,8},{8,9},{9,10},{10,1... | collective-permute-start | bytes 98312 | tf_op jit(solution)/shard_map/ppermute | solution.py:22
  122.1 1.3 collective-permute-start.1
  123.4 0.3 all-to-all-done.1
  123.7 0.7 reduce.3
  124.4 0.1 reshape.509
  124.5 0.1 reshape.482
  124.6 0.1 multiply_sine_fusion.1
  124.7 0.0 collective-permute-done
  124.7 3.2 %collective-permute-done.1 = f32[64,128]{1,0:T(8,128)S(1)} collective-permute-done((f32[64,128]{1,0:T(8,128)S(1)}, f32[64,128]{1,0:T(8,128)S(1)}, u32[]{:S(2)}, u32[]{:S(2)}) %collective-permute-start.1) | collective-permute-done | bytes 32800 | tf_op jit(solution)/shard_map/ppermute | solution.py:23
  127.9 25.8 %fusion.6 = f32[64,512]{1,0:T(8,128)S(1)} fusion(f32[512]{0:T(512)S(1)} %get-tuple-element.26, f32[512]{0:T(512)S(1)} %get-tuple-element.24, s32[512]{0:T(512)S(1)} %get-tuple-element.22, pred[512]{0:T(512)(128)(4,1)S(1)} %get-tuple-element.30, f32[64,128]{1,0:T(8,128)S(1)} %collective-permute-done.1, f32[32,6144]{1,0:T(8,128)S(1)} %get-tuple-element.15, ...), kind=kOutput, calls=%fused_computation.16 | convolution fusion | flops 2616115200 | bytes 1776128 | tf_op jit(solution)/shard_map/dot_general | solution.py:137
  153.7 0.0 copy-start.1
  153.7 0.0 copy-start.2
  153.7 26.1 %fusion.14 = f32[64,512]{1,0:T(8,128)S(1)} fusion(f32[512]{0:T(512)S(1)} %get-tuple-element.25, f32[512]{0:T(512)S(1)} %get-tuple-element.27, s32[512]{0:T(512)S(1)} %get-tuple-element.23, pred[512]{0:T(512)(128)(4,1)S(1)} %get-tuple-element.31, f32[64,128]{1,0:T(8,128)S(1)} %collective-permute-done.1, f32[32,6144]{1,0:T(8,128)S(1)} %get-tuple-element.15, ...), kind=kOutput, calls=%fused_computation.23 | convolution fusion | flops 2616115200 | bytes 1776128 | tf_op jit(solution)/shard_map/dot_general | solution.py:137
  179.8 0.2 copy.21
  180.0 0.3 reshape.510
  180.3 11.0 %all_to_all.20 = f32[8,1,8192]{2,1,0:T(1,128)S(1)} all-to-all(f32[8,1,8192]{2,1,0:T(1,128)S(1)} %reshape.510), channel_id=1, replica_groups=mesh['slab'=8,'term'=4] {'slab'}, dimensions={0} | all-to-all | bytes 524288 | tf_op jit(solution)/shard_map/all_to_all | solution.py:148
  191.3 0.5 broadcast.1603
  191.8 1.3 reduce.4
  193.1 0.2 reshape.511
  193.4 1.0 reshape.512
  194.4 5.7 %all-to-all-start.3 = ((f32[4,1,16384]{2,1,0:T(1,128)}), f32[4,1,16384]{2,1,0:T(1,128)S(1)}, u32[]{:S(2)}, u32[]{:S(2)}) async-start(f32[4,1,16384]{2,1,0:T(1,128)} %reshape.512), calls=%async_computation.3 | async-start | bytes 524288 | tf_op jit(solution)/shard_map/all_to_all | solution.py:147
  200.1 1.2 pad_maximum_fusion
  201.4 0.0 copy-done.1
  201.4 7.0 %all-to-all-done.3 = f32[4,1,16384]{2,1,0:T(1,128)S(1)} async-done(((f32[4,1,16384]{2,1,0:T(1,128)}), f32[4,1,16384]{2,1,0:T(1,128)S(1)}, u32[]{:S(2)}, u32[]{:S(2)}) %all-to-all-start.3) | async-done | bytes 262176 | tf_op jit(solution)/shard_map/all_to_all | solution.py:147
  208.3 1.4 reduce.5
  209.7 0.3 reshape.513
  210.0 1.0 gather_fusion
  211.1 0.0 copy-done.2
  211.1 0.1 select_bitcast_fusion
  211.2 0.8 copy.24
  (18 shorter events, 0.2 us)
Async XLA Ops:
  2.9 0.7 copy-start
  6.8 105.5 %all-to-all-start = ((s32[8,1,128]{2,1,0:T(1,128)}), s32[8,1,128]{2,1,0:T(1,128)}, u32[]{:S(2)}, u32[]{:S(2)}) async-start(s32[8,1,128]{2,1,0:T(1,128)} %reshape.506), calls=%async_computation | async-start | bytes 8192 | tf_op jit(solution)/shard_map/all_to_all | solution.py:115
  114.9 8.8 %all-to-all-start.1 = ((s32[4,1,256]{2,1,0:T(1,128)}), s32[4,1,256]{2,1,0:T(1,128)S(1)}, u32[]{:S(2)}, u32[]{:S(2)}) async-start(s32[4,1,256]{2,1,0:T(1,128)} %reshape.508), calls=%async_computation.1 | async-start | bytes 8192 | tf_op jit(solution)/shard_map/all_to_all | solution.py:114
  118.2 6.5 %collective-permute-start = (f32[64,128]{1,0:T(8,128)S(1)}, f32[64,128]{1,0:T(8,128)S(1)}, u32[]{:S(2)}, u32[]{:S(2)}) collective-permute-start(f32[64,128]{1,0:T(8,128)S(1)} %get-tuple-element.16), channel_id=1, source_target_pairs={{0,1},{1,2},{2,3},{3,4},{4,5},{5,6},{6,7},{7,8},{8,9},{9,10},{10,1... | collective-permute-start | bytes 98312 | tf_op jit(solution)/shard_map/ppermute | solution.py:22
  122.1 5.8 %collective-permute-start.1 = (f32[64,128]{1,0:T(8,128)S(1)}, f32[64,128]{1,0:T(8,128)S(1)}, u32[]{:S(2)}, u32[]{:S(2)}) collective-permute-start(f32[64,128]{1,0:T(8,128)S(1)} %get-tuple-element.17), channel_id=1, source_target_pairs={{1,0},{2,1},{3,2},{4,3},{5,4},{6,5},{7,6},{8,7},{9,8},{10,9},{11,1... | collective-permute-start | bytes 98312 | tf_op jit(solution)/shard_map/ppermute | solution.py:23
  153.7 47.7 %copy-start.1 = (s32[512,1]{0,1:T(1,128)S(1)}, s32[512,1]{0,1:T(1,128)}, u32[]{:S(2)}) copy-start(s32[512,1]{0,1:T(1,128)} %copy-done) | copy-start | bytes 6148
  153.7 57.4 %copy-start.2 = (pred[512]{0:T(512)(128)(4,1)S(1)}, pred[512]{0:T(512)(128)(4,1)}, u32[]{:S(2)}) copy-start(pred[512]{0:T(512)(128)(4,1)} %get-tuple-element.10) | copy-start | bytes 1540
  194.4 13.9 %all-to-all-start.3 = ((f32[4,1,16384]{2,1,0:T(1,128)}), f32[4,1,16384]{2,1,0:T(1,128)S(1)}, u32[]{:S(2)}, u32[]{:S(2)}) async-start(f32[4,1,16384]{2,1,0:T(1,128)} %reshape.512), calls=%async_computation.3 | async-start | bytes 524288 | tf_op jit(solution)/shard_map/all_to_all | solution.py:147
where the time goes:
time: 216 us; the launch traced here: 212 us
  matrix products  91.9 us (43%)
  other arithmetic  39.8 us (18%)
  blocking collectives  36.9 us (17%)
  starting transfers between devices  19.3 us (9%)
  local copies, waits for them, and re-layouts  12.7 us (6%)
  waiting for transfers between devices  10.5 us (5%)
    dot_general x2, matrix products, body(): lax.dot_general(extended, kernel, (((1,), (1,)), ((), ())), precision=lax...  51.8 us
    dot_general x1, matrix products, grid_terms(): jnp.dot(coeffs, basis_cos, precision=lax.Precision.HIGHEST, preferred_ele...  19.5 us
    dot_general x1, matrix products, grid_terms(): jnp.dot(coeffs, basis_sin, precision=lax.Precision.HIGHEST, preferred_ele...  19.5 us
    mul x1, other arithmetic, grid_terms(): jnp.sin(angle)[:, None, :] * cheb[None, :, :]  18.4 us
    all_gather x1, blocking collectives, body(): lax.all_gather(panels, 'term', axis=1, tiled=True)  14.4 us
    all_gather x1, blocking collectives, body(): lax.all_gather(block_phase, 'term', axis=1, tiled=True)  11.5 us
    all_to_all x1, blocking collectives, body(): lax.all_to_all(outgoing, 'slab', split_axis=1, concat_axis=1, tiled=True)  11 us
    sin x1, other arithmetic, grid_terms(): jnp.sin(angle)[:, None, :] * cheb[None, :, :]  7.04 us
  transfers between devices with their start and end apart: 5, of which 3 were waited for; matrix products, arithmetic and copies ran while one was open for 36% of the time, Pallas kernels for 0%

commit v1 on v0

v1 whole, which is shorter than its diff:
```python
import functools
import math

import jax
import jax.numpy as jnp
import ml_dtypes
import numpy as np
from jax import lax
from jax.experimental import pallas as pl
from jax.experimental.pallas import tpu as pltpu
from jax.sharding import PartitionSpec as P

TAPS = 256
OFFQ = 256
GS = 6144
PHASEQ = 4194304
TILE = 512
TILES = GS // TILE
WIN = 256
GROUP = 256
MESH = pl.DeviceIdType.MESH
F32 = jnp.float32
BF16 = jnp.bfloat16


def local_expansion(centers, half, order):
    nodes = np.cos((np.arange(order) + 0.5) * np.pi / order)
    back = np.cos(np.outer(np.arange(order), np.arccos(nodes))) * 2.0 / order
    back[0] *= 0.5
    x = np.asarray(centers, np.float64)[:, None] + half * nodes[None, :]
    tj = np.polynomial.chebyshev.chebvander(x, order - 1)
    return np.einsum("tnj,kn->tjk", tj, back)


def split_np(x):
    hi = x.astype(np.float32).astype(ml_dtypes.bfloat16)
    lo = (x - hi.astype(np.float64)).astype(np.float32).astype(ml_dtypes.bfloat16)
    return hi, lo


def local_cheb(width, order):
    y = (2.0 * np.arange(width) + 1.0) / width - 1.0
    return np.polynomial.chebyshev.chebvander(y, order - 1).T.astype(np.float32)


def tables(order, nblk):
    half = TILE / GS
    centers = (2.0 * TILE * np.arange(TILES) + TILE) / GS - 1.0
    m = local_expansion(centers, half, order)
    eye = np.eye(nblk)
    big = np.einsum("tjk,bc->tjbkc", m, eye).reshape(TILES, order * nblk, order * nblk)
    h = WIN / GS
    nodes = np.cos((np.arange(order) + 0.5) * np.pi / order)
    back = np.cos(np.outer(np.arange(order), np.arccos(nodes))) * 2.0 / order
    back[0] *= 0.5
    a_nodes = local_expansion(nodes * (1.0 - h), h, order)
    series = np.einsum("njk,mn->jkm", a_nodes, back).reshape(order * order, order)
    padded = np.zeros((order * order, 128), np.float64)
    padded[:, :order] = series
    return split_np(big), padded.astype(np.float32)


def split(x):
    hi = x.astype(BF16)
    return hi, (x - hi.astype(F32)).astype(BF16)


def dot3(ah, al, bh, bl):
    out = jnp.dot(ah, bh, preferred_element_type=F32)
    out = out + jnp.dot(al, bh, preferred_element_type=F32)
    return out + jnp.dot(ah, bl, preferred_element_type=F32)


def turned(x):
    half = x.shape[0] // 2
    return jnp.concatenate([-x[half:], x[:half]], 0)


def sincos(turns):
    turns = turns & (PHASEQ - 1)
    quad = (turns + PHASEQ // 8) >> 20
    r = (turns - (quad << 20)).astype(F32) * (2.0 * math.pi / PHASEQ)
    r2 = r * r
    s = r + r * r2 * (-1 / 6 + r2 * (1 / 120 + r2 * (-1 / 5040 + r2 * (1 / 362880))))
    c = 1.0 + r2 * (-0.5 + r2 * (1 / 24 + r2 * (-1 / 720 + r2 * (1 / 40320))))
    odd = (quad & 1) == 1
    sn = jnp.where(odd, c, s)
    cs = jnp.where(odd, s, c)
    sn = jnp.where((quad & 2) == 2, -sn, sn)
    cs = jnp.where(((quad + 1) & 2) == 2, -cs, cs)
    return sn, cs


def gather_kernel(n, pan_ref, ph_ref, pan_out, ph_out, own_sem, send_sem, recv_sem):
    me = lax.axis_index("term")
    barrier = pltpu.get_barrier_semaphore()
    for d in range(1, n):
        pl.semaphore_signal(barrier, inc=1, device_id={"term": lax.rem(me + d, n)}, device_id_type=MESH)
    pl.semaphore_wait(barrier, n - 1)
    pairs = ((pan_ref, pan_out), (ph_ref, ph_out))
    copies = []
    for d in range(1, n):
        for a, (src, dst) in enumerate(pairs):
            copy = pltpu.make_async_remote_copy(
                src_ref=src,
                dst_ref=dst.at[me],
                send_sem=send_sem.at[a, d],
                recv_sem=recv_sem.at[a, d],
                device_id={"term": lax.rem(me + d, n)},
                device_id_type=MESH,
            )
            copy.start()
            copies.append(copy)
    for a, (src, dst) in enumerate(pairs):
        own = pltpu.make_async_copy(src, dst.at[me], own_sem.at[a])
        own.start()
        copies.append(own)
    for copy in copies:
        copy.wait()


def gathered(n, pan, ph):
    return pl.pallas_call(
        functools.partial(gather_kernel, n),
        out_shape=(
            jax.ShapeDtypeStruct((n,) + pan.shape, pan.dtype),
            jax.ShapeDtypeStruct((n,) + ph.shape, ph.dtype),
        ),
        in_specs=[pl.BlockSpec(memory_space=pl.ANY)] * 2,
        out_specs=[pl.BlockSpec(memory_space=pl.ANY)] * 2,
        scratch_shapes=[
            pltpu.SemaphoreType.DMA((2,)),
            pltpu.SemaphoreType.DMA((2, n)),
            pltpu.SemaphoreType.DMA((2, n)),
        ],
        compiler_params=pltpu.CompilerParams(collective_id=0, has_side_effects=True),
    )(pan, ph)


def fill_basis(n, order, nblk, width, ph_ref, cheb_ref, hi_ref, lo_ref):
    lane = lax.broadcasted_iota(jnp.int32, (nblk, width), 1)

    def chunk(i, carry):
        adv = ph_ref[i, 8 : 8 + nblk, 128:129]
        sn, cs = sincos(lane * adv)
        for k in range(order):
            row = cheb_ref[k : k + 1, :]
            for part, wave in enumerate((cs, sn)):
                at = pl.multiple_of((i * 2 + part) * order * nblk + k * nblk, nblk)
                hi, lo = split(wave * row)
                hi_ref[pl.ds(at, nblk), :] = hi
                lo_ref[pl.ds(at, nblk), :] = lo
        return carry

    lax.fori_loop(0, n, chunk, 0)


def grid_kernel(n, order, nblk, pan_ref, ph_ref, cheb_ref, mh_ref, ml_ref, out_ref, bh, bl, ah, al):
    cols = order * nblk
    rows = pan_ref.shape[1]
    device = lax.axis_index("slab") * n + lax.axis_index("term")
    base = device * GS
    fill_basis(n, order, nblk, TILE, ph_ref, cheb_ref, bh, bl)

    def chunk(i, carry):
        ph, pl_ = split(pan_ref[i])
        p0 = ph_ref[i, 0:1, :]
        adv = ph_ref[i, 1:2, :]

        def tile(t, c2):
            z = dot3(ph, pl_, mh_ref[t], ml_ref[t])
            sn, cs = sincos(p0 + (base + t * TILE) * adv)
            q = cs * z + sn * turned(z)
            hi, lo = split(q)
            at = pl.multiple_of(t * rows, rows)
            c0 = pl.multiple_of(i * 2 * cols, 2 * cols)
            ah[pl.ds(at, rows), pl.ds(c0, cols)] = hi
            al[pl.ds(at, rows), pl.ds(c0, cols)] = lo
            c1 = pl.multiple_of(c0 + cols, cols)
            hi2, lo2 = split(turned(q))
            ah[pl.ds(at, rows), pl.ds(c1, cols)] = hi2
            al[pl.ds(at, rows), pl.ds(c1, cols)] = lo2
            return c2

        return lax.fori_loop(0, TILES, tile, carry)

    lax.fori_loop(0, n, chunk, 0)
    mrows = 4 * rows
    for lo_col in range(0, TILE, 256):
        for mb in range(TILES // 4):
            rr = slice(mb * mrows, (mb + 1) * mrows)
            cc = slice(lo_col, lo_col + 256)
            acc = dot3(ah[rr, :], al[rr, :], bh[:, cc], bl[:, cc])
            for t in range(4):
                start = (mb * 4 + t) * TILE + lo_col
                out_ref[:, start : start + 256] = acc[t * rows : (t + 1) * rows]


def target_kernel(
    n, n_dev, order, nblk, pan_ref, ph_ref, cheb_ref, series_ref, own_ref, cell_ref, off_ref, out_ref,
    eh, el, wh, wl, a_ref, u_ref, vh, vl, s_ref,
):
    cols = order * nblk

    @pl.when(pl.program_id(0) == 0)
    def _():
        fill_basis(n, order, nblk, WIN, ph_ref, cheb_ref, eh, el)

    owner = own_ref[...]
    cell = cell_ref[...]
    frac = (off_ref[...].astype(F32) + 0.5) * (1.0 / OFFQ)
    left = cell - (TAPS // 2 - 1) < 0
    right = cell + TAPS // 2 >= GS
    out_ref[...] = jnp.zeros_like(out_ref)

    def piece(slab, start, valid):
        shift = (slab - owner) * GS + start - cell + (TAPS // 2 - 1)
        tap = lax.broadcasted_iota(jnp.int32, (WIN, GROUP), 0)
        place = tap + shift
        inside = (place >= 0) & (place < TAPS) & valid
        dist = (place - TAPS // 2 + 1).astype(F32) - frac
        sgn = jnp.where((place & 1) == 0, 1.0, -1.0)
        sn, _ = sincos((off_ref[...] * 2 + 1) * (PHASEQ // (4 * OFFQ)))
        weights = sgn * sn / (math.pi * dist) * jnp.exp(dist * dist * (-18.0 / (TAPS * TAPS)))
        hi, lo = split(jnp.where(inside, weights, 0.0))
        wh[...] = hi
        wl[...] = lo
        center = (2 * start + WIN - GS).astype(F32) / float(GS - WIN)
        rows = [jnp.ones_like(center), center]
        for j in range(2, order):
            rows.append(2.0 * center * rows[-1] - rows[-2])
        s_ref[...] = jnp.zeros_like(s_ref)
        for j in range(order):
            s_ref[j : j + 1, :] = rows[j]
        a_ref[...] = jnp.dot(
            series_ref[...], s_ref[...], precision=lax.Precision.HIGHEST, preferred_element_type=F32
        )
        first = slab * GS + start

        def chunk(i, carry):
            at = pl.multiple_of(i * 2 * cols, 2 * cols)
            u_ref[...] = dot3(eh[pl.ds(at, 2 * cols), :], el[pl.ds(at, 2 * cols), :], wh[...], wl[...])
            p0 = ph_ref[i, 8 : 8 + nblk, 0:1]
            adv = ph_ref[i, 8 : 8 + nblk, 128:129]
            sn, cs = sincos(p0 + first * adv)
            for b0 in range(0, nblk, 8):
                for l0 in range(0, GROUP, 128):
                    ll = slice(l0, l0 + 128)
                    uc = [u_ref[k * nblk + b0 : k * nblk + b0 + 8, ll] for k in range(order)]
                    us = [u_ref[cols + k * nblk + b0 : cols + k * nblk + b0 + 8, ll] for k in range(order)]
                    s8 = sn[b0 : b0 + 8, ll]
                    c8 = cs[b0 : b0 + 8, ll]
                    for j in range(order):
                        vc = vs = None
                        for k in range(j + 1):
                            a = a_ref[j * order + k : j * order + k + 1, ll]
                            vc = a * uc[k] if vc is None else vc + a * uc[k]
                            vs = a * us[k] if vs is None else vs + a * us[k]
                        u_j = j * nblk + b0
                        s_re = c8 * vc - s8 * vs
                        s_im = s8 * vc + c8 * vs
                        vh[u_j : u_j + 8, ll] = s_re
                        vl[u_j : u_j + 8, ll] = s_im
            ph, pl_ = split(pan_ref[i])
            th, tl = turned(ph), turned(pl_)
            rh, rl = split(vh[...])
            ih, il = split(vl[...])
            out_ref[...] += dot3(ph, pl_, rh, rl) + dot3(th, tl, ih, il)
            return carry

        lax.fori_loop(0, n, chunk, 0)

    start = jnp.clip(cell - (TAPS // 2 - 1), 0, GS - WIN)
    piece(owner, start, jnp.full(cell.shape, True))
    side_ok = (left & (owner > 0)) | (right & (owner < n_dev - 1))

    @pl.when(jnp.max(side_ok.astype(jnp.int32)) > 0)
    def _():
        slab = jnp.where(left, owner - 1, owner + 1)
        piece(slab, jnp.where(left, GS - WIN, 0), side_ok)


def body(n_slab, n, panels, block_phase, target_owner, target_cell, target_offset):
    n_dev = n_slab * n
    channels = panels.shape[0]
    nblk = block_phase.shape[1]
    order = panels.shape[1] // nblk
    cols = order * nblk
    targets = target_cell.shape[0]
    (mh, ml), series = tables(order, nblk)
    pan = panels.reshape(channels, nblk, order).swapaxes(1, 2).reshape(channels, cols)
    wide = jnp.tile(block_phase, (1, order))
    tall = jnp.repeat(block_phase.T, cols // 2, axis=1)
    ph = jnp.concatenate([wide, jnp.zeros((6, cols), jnp.int32), tall], 0)
    pan, ph = gathered(n, pan, ph)
    vmem = pl.BlockSpec(memory_space=pltpu.VMEM)
    grid = pl.pallas_call(
        functools.partial(grid_kernel, n, order, nblk),
        out_shape=jax.ShapeDtypeStruct((channels, GS), F32),
        in_specs=[vmem] * 5,
        out_specs=vmem,
        scratch_shapes=[
            pltpu.VMEM((n * 2 * cols, TILE), BF16),
            pltpu.VMEM((n * 2 * cols, TILE), BF16),
            pltpu.VMEM((TILES * channels, n * 2 * cols), BF16),
            pltpu.VMEM((TILES * channels, n * 2 * cols), BF16),
        ],
        compiler_params=pltpu.CompilerParams(vmem_limit_bytes=48 << 20),
    )(pan, ph, local_cheb(TILE, order), mh, ml)
    lanes = pl.BlockSpec((1, GROUP), lambda g: (0, g))
    values = pl.pallas_call(
        functools.partial(target_kernel, n, n_dev, order, nblk),
        out_shape=jax.ShapeDtypeStruct((channels, targets), F32),
        grid=(targets // GROUP,),
        in_specs=[
            pl.BlockSpec((n, channels, cols), lambda g: (0, 0, 0)),
            pl.BlockSpec(ph.shape, lambda g: (0, 0, 0)),
            pl.BlockSpec((order, WIN), lambda g: (0, 0)),
            pl.BlockSpec(series.shape, lambda g: (0, 0)),
            lanes,
            lanes,
            lanes,
        ],
        out_specs=pl.BlockSpec((channels, GROUP), lambda g: (0, g)),
        scratch_shapes=[
            pltpu.VMEM((n * 2 * cols, WIN), BF16),
            pltpu.VMEM((n * 2 * cols, WIN), BF16),
            pltpu.VMEM((WIN, GROUP), BF16),
            pltpu.VMEM((WIN, GROUP), BF16),
            pltpu.VMEM((order * order, GROUP), F32),
            pltpu.VMEM((2 * cols, GROUP), F32),
            pltpu.VMEM((cols, GROUP), F32),
            pltpu.VMEM((cols, GROUP), F32),
            pltpu.VMEM((128, GROUP), F32),
        ],
        compiler_params=pltpu.CompilerParams(vmem_limit_bytes=48 << 20),
    )(
        pan,
        ph,
        local_cheb(WIN, order),
        series,
        target_owner.reshape(1, targets),
        target_cell.reshape(1, targets),
        target_offset.reshape(1, targets),
    )
    return grid, values


def solution(mesh):
    placed = (
        P(None, "term"),
        P(None, "term"),
        P(("slab", "term"), None),
        P(("slab", "term")),
        P(("slab", "term")),
    )
    return jax.shard_map(
        functools.partial(body, mesh.shape["slab"], mesh.shape["term"]),
        mesh=mesh,
        in_specs=placed,
        out_specs=(P(None, ("slab", "term")), P(None, ("slab", "term"))),
        check_vma=False,
    )
```

time: 216 us -> 64.6 us (0.30); the launches traced: 212 us -> 64.1 us
  matrix products: 91.9 us -> 0 us
  Pallas kernels: 0 us -> 51 us
  other arithmetic: 39.8 us -> 0.68 us
  blocking collectives: 36.9 us -> 0 us
  starting transfers between devices: 19.3 us -> 0 us
  waiting for transfers between devices: 10.5 us -> 0 us
    dot_general x5 -> x0, matrix products: 91.9 us -> none  [the longest x2 51.8 us: body(): lax.dot_general(extended, kernel, (((1,), (1,)), ((), ())), precision=lax...]
    pallas_call x0 -> x3, Pallas kernels: none -> 51 us  [the longest x1 20.8 us: body(): pl.pallas_call(functools.partial(target_kernel, n, n_dev, order, nblk), o...]
    all_gather x2 -> x0, blocking collectives: 25.9 us -> none  [the longest x1 14.4 us: body(): lax.all_gather(panels, 'term', axis=1, tiled=True)]
    mul x1 -> x0, other arithmetic: 18.4 us -> none  [grid_terms(): jnp.sin(angle)[:, None, :] * cheb[None, :, :]]
    all_to_all x3 -> x0, starting transfers between devices: 14.1 us -> none  [the longest x1 5.71 us: body(): lax.all_to_all(lax.all_to_all(outgoing, 'slab', split_axis=1, concat_axis...]
    all_to_all x1 -> x0, blocking collectives: 11 us -> none  [body(): lax.all_to_all(outgoing, 'slab', split_axis=1, concat_axis=1, tiled=True)]
    all_to_all x3 -> x0, waiting for transfers between devices: 7.31 us -> none  [the longest x1 6.96 us: body(): lax.all_to_all(lax.all_to_all(outgoing, 'slab', split_axis=1, concat_axis...]
    sin x2 -> x0, other arithmetic: 7.09 us -> none  [the longest x1 7.04 us: grid_terms(): jnp.sin(angle)[:, None, :] * cheb[None, :, :]]
  transfers between devices with their start and end apart: 5 -> 0, of which waited for: 3 -> 0; matrix products, arithmetic and copies ran while one was open for 36% -> 0% of each run, Pallas kernels for 0% -> 0%
where the time goes in v1:
time: 64.6 us; the launch traced here: 64.1 us
  Pallas kernels  51 us (79%)
  local copies, waits for them, and re-layouts  11.7 us (18%)
  between operations  0.69 us (1%)
  other arithmetic  0.68 us (1%)
    pallas_call x1, Pallas kernels, body(): pl.pallas_call(functools.partial(target_kernel, n, n_dev, order, nblk), o...  20.8 us
    pallas_call x1, Pallas kernels, body(): pl.pallas_call(functools.partial(grid_kernel, n, order, nblk), out_shape=...  17.9 us
    pallas_call x1, Pallas kernels, gathered(): pl.pallas_call(functools.partial(gather_kernel, n), out_shape=(jax.ShapeD...  12.3 us
    unnamed x22, local copies, waits for them, and re-layouts  9.26 us

profile of v1, /device:TPU:0, one launch (start us, length us, event | category | flops | bytes accessed | tf_op | source)
XLA Modules:
  0.0 64.1 jit_solution(12897177416885183961)
XLA Ops:
  0.6 0.0 copy-start.5
  0.7 0.1 pad.1.clone
  0.7 0.8 %copy.16 = s32[16,2]{1,0:T(8,128)S(1)} copy(s32[16,2]{0,1:T(2,128)} %bitcast.19) | data formatting | bytes 256 | tf_op jit(solution)/shard_map/transpose | solution.py:293
  1.5 0.1 broadcast_in_dim.7
  1.6 0.7 %tile.4 = s32[2,16,16]{2,1,0:T(8,128)S(1)} broadcast(s32[2,16]{1,0:T(2,128)} %param.11), dimensions={0,2} | broadcast | bytes 2176 | tf_op jit(solution)/shard_map/tile | solution.py:292
  2.3 0.1 tile.10
  2.3 0.7 %pad_add_fusion.ph_ref = s32[24,256]{1,0:T(8,128)} fusion(s32[16,256]{1,0:T(8,128)S(1)} %bitcast.17, s32[2,256]{1,0:T(2,128)S(1)} %tile.10, s32[24]{0:T(128)S(1)} %pad.1.clone), kind=kLoop, calls=%fused_computation | loop fusion | flops 12288 | bytes 43104 | tf_op jit(solution)/shard_map/concatenate | solution.py:294
  3.0 0.9 %copy.14 = f32[64,256]{0,1:T(8,128)S(1)} copy(f32[64,256]{1,0:T(8,128)} %param.10) | data formatting | bytes 131072 | tf_op args[0]
  4.0 0.7 %copy.17.pan_ref = f32[64,256]{1,0:T(8,128)} copy(f32[64,256]{0,1:T(8,128)S(1)} %bitcast.15) | data formatting | bytes 131072 | tf_op jit(solution)/shard_map/reshape | solution.py:291
  4.7 12.3 %shard_map.113 = (f32[4,64,256]{2,1,0:T(8,128)}, s32[4,24,256]{2,1,0:T(8,128)}) custom-call(f32[64,256]{1,0:T(8,128)} %copy.17.pan_ref, s32[24,256]{1,0:T(8,128)} %pad_add_fusion.ph_ref), custom_call_target="tpu_custom_call" | custom-call | tf_op jit(solution)/shard_map/pallas_call | solution.py:123
  17.0 0.0 copy-start.2
  17.0 0.9 %copy-done.2 = f32[4,64,256]{2,1,0:T(8,128)S(1)} copy-done((f32[4,64,256]{2,1,0:T(8,128)S(1)}, f32[4,64,256]{2,1,0:T(8,128)}, u32[]{:S(2)}) %copy-start.2) | copy-done | bytes 262168
  18.0 0.0 copy-start.3
  18.0 0.9 %copy-done.3 = s32[4,24,256]{2,1,0:T(8,128)S(1)} copy-done((s32[4,24,256]{2,1,0:T(8,128)S(1)}, s32[4,24,256]{2,1,0:T(8,128)}, u32[]{:S(2)}) %copy-start.3) | copy-done | bytes 98328
  18.8 0.0 copy-start.4
  18.8 0.9 %copy-done.4 = f32[256,128]{1,0:T(8,128)S(1)} copy-done((f32[256,128]{1,0:T(8,128)S(1)}, f32[256,128]{1,0:T(8,128)}, u32[]{:S(2)}) %copy-start.4) | copy-done | bytes 131096
  19.8 0.0 copy-start.6
  19.8 0.7 %copy-done.6 = f32[16,256]{1,0:T(8,128)S(1)} copy-done((f32[16,256]{1,0:T(8,128)S(1)}, f32[16,256]{1,0:T(8,128)}, u32[]{:S(2)}) %copy-start.6) | copy-done | bytes 16408
  20.5 0.0 copy-start.7
  20.5 0.7 %copy-done.7 = s32[512,1]{0,1:T(1,128)S(1)} copy-done((s32[512,1]{0,1:T(1,128)S(1)}, s32[512,1]{0,1:T(1,128)}, u32[]{:S(2)}) %copy-start.7) | copy-done | bytes 2072
  21.2 0.0 copy-start.8
  21.2 0.7 %copy-done.8 = s32[512]{0:T(512)S(1)} copy-done((s32[512]{0:T(512)S(1)}, s32[512]{0:T(512)}, u32[]{:S(2)}) %copy-start.8) | copy-done | bytes 2072
  21.8 0.0 copy-start.9
  21.8 0.7 %copy-done.9 = s32[512]{0:T(512)S(1)} copy-done((s32[512]{0:T(512)S(1)}, s32[512]{0:T(512)}, u32[]{:S(2)}) %copy-start.9) | copy-done | bytes 2072
  22.5 20.8 %shard_map.115 = f32[64,512]{1,0:T(8,128)} custom-call(f32[4,64,256]{2,1,0:T(8,128)S(1)} %copy-done.2, s32[4,24,256]{2,1,0:T(8,128)S(1)} %copy-done.3, f32[16,256]{1,0:T(8,128)S(1)} %copy-done.6, f32[256,128]{1,0:T(8,128)S(1)} %copy-done.4, s32[1,512]{1,0:T(1,128)S(1)} %bitcast.12, s32[1,512]{1,0:T(1,128)S(1)} %bitcast.13, s32[1,512]{1,0:T(1,128)S(1)} %bitcast.14), custom_call_target="tpu_custom_call" | custom-call | tf_op jit(solution)/shard_map/pallas_call | solution.py:311
  43.3 0.0 copy-done.5
  43.3 0.0 copy-start
  43.3 1.4 %copy-done = bf16[12,256,256]{2,1,0:T(8,128)(2,1)S(1)} copy-done((bf16[12,256,256]{2,1,0:T(8,128)(2,1)S(1)}, bf16[12,256,256]{2,1,0:T(8,128)(2,1)}, u32[]{:S(2)}) %copy-start) | copy-done | bytes 1572888
  44.7 0.0 copy-start.1
  44.7 1.4 %copy-done.1 = bf16[12,256,256]{2,1,0:T(8,128)(2,1)S(1)} copy-done((bf16[12,256,256]{2,1,0:T(8,128)(2,1)S(1)}, bf16[12,256,256]{2,1,0:T(8,128)(2,1)}, u32[]{:S(2)}) %copy-start.1) | copy-done | bytes 1572888
  46.1 17.9 %shard_map.114 = f32[64,6144]{1,0:T(8,128)} custom-call(f32[4,64,256]{2,1,0:T(8,128)S(1)} %copy-done.2, s32[4,24,256]{2,1,0:T(8,128)S(1)} %copy-done.3, f32[16,512]{1,0:T(8,128)S(1)} %copy-done.5, bf16[12,256,256]{2,1,0:T(8,128)(2,1)S(1)} %copy-done.1, bf16[12,256,256]{2,1,0:T(8,128)(2,1)S(1)} %copy-done), custom_call_target="tpu_custom_call" | custom-call | tf_op jit(solution)/shard_map/pallas_call | solution.py:297
  (3 shorter events, 0.1 us)
Async XLA Ops:
  0.6 42.7 %copy-start.5 = (f32[16,512]{1,0:T(8,128)S(1)}, f32[16,512]{1,0:T(8,128)}, u32[]{:S(2)}) copy-start(f32[16,512]{1,0:T(8,128)} %constant.12.clone.cheb_ref) | copy-start | bytes 98308
  17.0 1.0 %copy-start.2 = (f32[4,64,256]{2,1,0:T(8,128)S(1)}, f32[4,64,256]{2,1,0:T(8,128)}, u32[]{:S(2)}) copy-start(f32[4,64,256]{2,1,0:T(8,128)} %get-tuple-element.4.pan_ref) | copy-start | bytes 786436
  18.0 0.9 %copy-start.3 = (s32[4,24,256]{2,1,0:T(8,128)S(1)}, s32[4,24,256]{2,1,0:T(8,128)}, u32[]{:S(2)}) copy-start(s32[4,24,256]{2,1,0:T(8,128)} %get-tuple-element.5.ph_ref) | copy-start | bytes 294916
  18.8 0.9 %copy-start.4 = (f32[256,128]{1,0:T(8,128)S(1)}, f32[256,128]{1,0:T(8,128)}, u32[]{:S(2)}) copy-start(f32[256,128]{1,0:T(8,128)} %constant.16.clone.series_ref) | copy-start | bytes 393220
  19.8 0.7 %copy-start.6 = (f32[16,256]{1,0:T(8,128)S(1)}, f32[16,256]{1,0:T(8,128)}, u32[]{:S(2)}) copy-start(f32[16,256]{1,0:T(8,128)} %constant.15.clone.cheb_ref) | copy-start | bytes 49156
  20.5 0.7 %copy-start.7 = (s32[512,1]{0,1:T(1,128)S(1)}, s32[512,1]{0,1:T(1,128)}, u32[]{:S(2)}) copy-start(s32[512,1]{0,1:T(1,128)} %param.12) | copy-start | bytes 6148
  21.2 0.7 %copy-start.8 = (s32[512]{0:T(512)S(1)}, s32[512]{0:T(512)}, u32[]{:S(2)}) copy-start(s32[512]{0:T(512)} %param.13) | copy-start | bytes 6148
  21.8 0.7 %copy-start.9 = (s32[512]{0:T(512)S(1)}, s32[512]{0:T(512)}, u32[]{:S(2)}) copy-start(s32[512]{0:T(512)} %param.14) | copy-start | bytes 6148
  43.3 1.4 %copy-start = (bf16[12,256,256]{2,1,0:T(8,128)(2,1)S(1)}, bf16[12,256,256]{2,1,0:T(8,128)(2,1)}, u32[]{:S(2)}) copy-start(bf16[12,256,256]{2,1,0:T(8,128)(2,1)} %constant.14.clone.ml_ref) | copy-start | bytes 4718596
  44.7 1.4 %copy-start.1 = (bf16[12,256,256]{2,1,0:T(8,128)(2,1)S(1)}, bf16[12,256,256]{2,1,0:T(8,128)(2,1)}, u32[]{:S(2)}) copy-start(bf16[12,256,256]{2,1,0:T(8,128)(2,1)} %constant.13.clone.mh_ref) | copy-start | bytes 4718596

commit v2 on v1

v2 whole, which is shorter than its diff:
```python
import functools
import math

import jax
import jax.numpy as jnp
import ml_dtypes
import numpy as np
from jax import lax
from jax.experimental import pallas as pl
from jax.experimental.pallas import tpu as pltpu
from jax.sharding import PartitionSpec as P

TAPS = 256
OFFQ = 256
GS = 6144
PHASEQ = 4194304
TILE = 1024
TILES = GS // TILE
WIN = 256
GROUP = 256
SIDE = 128
MESH = pl.DeviceIdType.MESH
F32 = jnp.float32
BF16 = jnp.bfloat16


def local_expansion(centers, half, order):
    nodes = np.cos((np.arange(order) + 0.5) * np.pi / order)
    back = np.cos(np.outer(np.arange(order), np.arccos(nodes))) * 2.0 / order
    back[0] *= 0.5
    x = np.asarray(centers, np.float64)[:, None] + half * nodes[None, :]
    tj = np.polynomial.chebyshev.chebvander(x, order - 1)
    return np.einsum("tnj,kn->tjk", tj, back)


def split_np(x):
    hi = x.astype(np.float32).astype(ml_dtypes.bfloat16)
    lo = (x - hi.astype(np.float64)).astype(np.float32).astype(ml_dtypes.bfloat16)
    return hi, lo


def local_cheb(width, order):
    y = (2.0 * np.arange(width) + 1.0) / width - 1.0
    return np.polynomial.chebyshev.chebvander(y, order - 1).T.astype(np.float32)


def tables(order, nblk):
    half = TILE / GS
    centers = (2.0 * TILE * np.arange(TILES) + TILE) / GS - 1.0
    m = local_expansion(centers, half, order)
    eye = np.eye(nblk)
    big = np.einsum("tjk,bc->tbjkc", m, eye).reshape(TILES, order * nblk, order * nblk)
    h = WIN / GS
    nodes = np.cos((np.arange(order) + 0.5) * np.pi / order)
    back = np.cos(np.outer(np.arange(order), np.arccos(nodes))) * 2.0 / order
    back[0] *= 0.5
    a_nodes = local_expansion(nodes * (1.0 - h), h, order)
    series = np.einsum("njk,mn->jkm", a_nodes, back).reshape(order * order, order)
    padded = np.zeros((order * order, 128), np.float64)
    padded[:, :order] = series
    return split_np(big), padded.astype(np.float32)


def split(x):
    hi = x.astype(BF16)
    return hi, (x - hi.astype(F32)).astype(BF16)


def dot3(ah, al, bh, bl):
    out = jnp.dot(ah, bh, preferred_element_type=F32)
    out = out + jnp.dot(al, bh, preferred_element_type=F32)
    return out + jnp.dot(ah, bl, preferred_element_type=F32)


def turned(x):
    half = x.shape[0] // 2
    return jnp.concatenate([-x[half:], x[:half]], 0)


def sincos(turns):
    turns = turns & (PHASEQ - 1)
    quad = (turns + PHASEQ // 8) >> 20
    r = (turns - (quad << 20)).astype(F32) * (2.0 * math.pi / PHASEQ)
    r2 = r * r
    s = r + r * r2 * (-1 / 6 + r2 * (1 / 120 + r2 * (-1 / 5040 + r2 * (1 / 362880))))
    c = 1.0 + r2 * (-0.5 + r2 * (1 / 24 + r2 * (-1 / 720 + r2 * (1 / 40320))))
    odd = (quad & 1) == 1
    sn = jnp.where(odd, c, s)
    cs = jnp.where(odd, s, c)
    sn = jnp.where((quad & 2) == 2, -sn, sn)
    cs = jnp.where(((quad + 1) & 2) == 2, -cs, cs)
    return sn, cs


def gather_kernel(n, pan_ref, ph_ref, pan_out, ph_out, own_sem, send_sem, recv_sem, pass_sem, got_sem):
    me = lax.axis_index("term")
    slab = lax.axis_index("slab")
    core = lax.rem(slab, 2)
    twin = {"slab": slab + 1 - 2 * core}
    half = pan_ref.shape[0] // 2
    mine = pl.ds(pl.multiple_of(core * half, half), half)
    barrier = pltpu.get_barrier_semaphore()
    for d in range(1, n):
        pl.semaphore_signal(barrier, inc=1, device_id={"term": lax.rem(me + d, n)}, device_id_type=MESH)
    pl.semaphore_signal(barrier, inc=1, device_id=twin, device_id_type=MESH)
    pl.semaphore_wait(barrier, n)
    arriving = []
    rest = []
    for d in sorted(range(1, n), key=lambda d: -min(d, n - d)):
        peer = {"term": lax.rem(me + d, n)}
        big = pltpu.make_async_remote_copy(
            src_ref=pan_ref.at[mine],
            dst_ref=pan_out.at[me, mine],
            send_sem=send_sem.at[0, d],
            recv_sem=recv_sem.at[0, d],
            device_id=peer,
            device_id_type=MESH,
        )
        small = pltpu.make_async_remote_copy(
            src_ref=ph_ref,
            dst_ref=ph_out.at[me],
            send_sem=send_sem.at[1, d],
            recv_sem=recv_sem.at[1, d],
            device_id=peer,
            device_id_type=MESH,
        )
        big.start()
        small.start()
        arriving.append((d, big))
        rest.append(small)
    for a, (src, dst) in enumerate(((pan_ref, pan_out), (ph_ref, ph_out))):
        own = pltpu.make_async_copy(src, dst.at[me], own_sem.at[a])
        own.start()
        rest.append(own)
    for d, big in reversed(arriving):
        big.wait_recv()
        origin = lax.rem(me - d + n, n)
        passed = pltpu.make_async_remote_copy(
            src_ref=pan_out.at[origin, mine],
            dst_ref=pan_out.at[origin, mine],
            send_sem=pass_sem.at[d],
            recv_sem=got_sem.at[d],
            device_id=twin,
            device_id_type=MESH,
        )
        passed.start()
        rest.append(passed)
    for _, big in arriving:
        big.wait_send()
    for copy in rest:
        copy.wait()


def gathered(n, pan, ph):
    return pl.pallas_call(
        functools.partial(gather_kernel, n),
        out_shape=(
            jax.ShapeDtypeStruct((n,) + pan.shape, pan.dtype),
            jax.ShapeDtypeStruct((n,) + ph.shape, ph.dtype),
        ),
        in_specs=[pl.BlockSpec(memory_space=pl.ANY)] * 2,
        out_specs=[pl.BlockSpec(memory_space=pl.ANY)] * 2,
        scratch_shapes=[
            pltpu.SemaphoreType.DMA((2,)),
            pltpu.SemaphoreType.DMA((2, n)),
            pltpu.SemaphoreType.DMA((2, n)),
            pltpu.SemaphoreType.DMA((n,)),
            pltpu.SemaphoreType.DMA((n,)),
        ],
        compiler_params=pltpu.CompilerParams(collective_id=0, has_side_effects=True),
    )(pan, ph)


def spread_phases(n, order, nblk, ph_ref, col_ref, row_ref):
    cols = order * nblk
    pick = (
        lax.broadcasted_iota(jnp.int32, (nblk, cols), 1) % nblk
        == lax.broadcasted_iota(jnp.int32, (nblk, cols), 0)
    ).astype(F32)
    eye = pick[:, :nblk]
    for i in range(n):
        values = ph_ref[i].astype(F32)
        row = jnp.dot(values, pick, precision=lax.Precision.HIGHEST, preferred_element_type=F32)
        row_ref[i, 0:2] = row.astype(jnp.int32)
        col = lax.dot_general(
            eye, values, (((1,), (1,)), ((), ())), precision=lax.Precision.HIGHEST, preferred_element_type=F32
        ).astype(jnp.int32)
        col_ref[i, :, 0:128] = jnp.broadcast_to(col[:, 0:1], (nblk, 128))
        col_ref[i, :, 128:256] = jnp.broadcast_to(col[:, 1:2], (nblk, 128))


def fill_basis(n, order, nblk, width, col_ref, cheb_ref, hi_ref, lo_ref):
    lane = lax.broadcasted_iota(jnp.int32, (nblk, width), 1)

    def chunk(i, carry):
        sn, cs = sincos(lane * col_ref[i, :, 128:129])
        for k in range(order):
            row = cheb_ref[k : k + 1, :]
            for part, wave in enumerate((cs, sn)):
                at = pl.multiple_of((i * 2 + part) * order * nblk + k * nblk, nblk)
                hi, lo = split(wave * row)
                hi_ref[pl.ds(at, nblk), :] = hi
                lo_ref[pl.ds(at, nblk), :] = lo
        return carry

    lax.fori_loop(0, n, chunk, 0)


def work_kernel(
    n, n_dev, order, nblk,
    pan_ref, ph_ref, cheb_ref, wcheb_ref, series_ref, own_ref, cell_ref, off_ref, mh_hbm, ml_hbm,
    grid_out, val_ref,
    m_ref, load_sem, store_sem, col_ref, row_ref, bh, bl, ah, al, grid_ref,
    eh, el, wh, wl, a_ref, u_ref, vr, vi, s_ref, pp, acc_ref,
):
    cols = order * nblk
    rows = pan_ref.shape[1]
    count = own_ref.shape[1]
    loads = [pltpu.make_async_copy(src, m_ref.at[a], load_sem.at[a]) for a, src in enumerate((mh_hbm, ml_hbm))]
    for copy in loads:
        copy.start()
    spread_phases(n, order, nblk, ph_ref, col_ref, row_ref)
    fill_basis(n, order, nblk, TILE, col_ref, cheb_ref, bh, bl)
    fill_basis(n, order, nblk, WIN, col_ref, wcheb_ref, eh, el)
    device = lax.axis_index("slab") * n + lax.axis_index("term")
    base = device * GS
    r = lax.broadcasted_iota(jnp.int32, (cols, cols), 0)
    c = lax.broadcasted_iota(jnp.int32, (cols, cols), 1)
    perm = ((r % order == c // nblk) & (r // order == c % nblk)).astype(F32).astype(BF16)
    for copy in loads:
        copy.wait()

    def grid_chunk(i, carry):
        both = jnp.concatenate(split(pan_ref[i]), 0)
        pp[i] = jnp.dot(both, perm, preferred_element_type=F32).astype(BF16)
        p0 = row_ref[i, 0:1, :]
        adv = row_ref[i, 1:2, :]
        c0 = pl.multiple_of(i * 2 * cols, 2 * cols)
        c1 = pl.multiple_of(c0 + cols, cols)
        for t in range(TILES):
            z2 = jnp.dot(both, m_ref[0, t], preferred_element_type=F32)
            z = z2[:rows] + z2[rows:] + jnp.dot(both[:rows], m_ref[1, t], preferred_element_type=F32)
            sn, cs = sincos(p0 + (base + t * TILE) * adv)
            q = cs * z + sn * turned(z)
            hi, lo = split(q)
            rr = slice(t * rows, (t + 1) * rows)
            ah[rr, pl.ds(c0, cols)] = hi
            al[rr, pl.ds(c0, cols)] = lo
            ah[rr, pl.ds(c1, cols)] = turned(hi)
            al[rr, pl.ds(c1, cols)] = turned(lo)
        return carry

    lax.fori_loop(0, n, grid_chunk, 0)
    for lo_col in range(0, TILE, 256):
        cc = slice(lo_col, lo_col + 256)
        acc = dot3(ah[...], al[...], bh[:, cc], bl[:, cc])
        for t in range(TILES):
            start = t * TILE + lo_col
            grid_ref[:, start : start + 256] = acc[t * rows : (t + 1) * rows]
    store = pltpu.make_async_copy(grid_ref, grid_out, store_sem)
    store.start()

    def piece(width, owner, cell, offset, slab, start, valid):
        full = slice(0, width)
        shift = (slab - owner) * GS + start - cell + (TAPS // 2 - 1)
        frac = (offset.astype(F32) + 0.5) * (1.0 / OFFQ)
        place = lax.broadcasted_iota(jnp.int32, (WIN, width), 0) + shift
        inside = (place >= 0) & (place < TAPS) & valid
        dist = (place - TAPS // 2 + 1).astype(F32) - frac
        sgn = jnp.where((place & 1) == 0, 1.0, -1.0)
        sn, _ = sincos((offset * 2 + 1) * (PHASEQ // (4 * OFFQ)))
        weights = sgn * sn / (math.pi * dist) * jnp.exp(dist * dist * (-18.0 / (TAPS * TAPS)))
        hi, lo = split(jnp.where(inside, weights, 0.0))
        wh[:, full] = hi
        wl[:, full] = lo
        center = (2 * start + WIN - GS).astype(F32) / float(GS - WIN)
        tm = [jnp.ones_like(center), center]
        for j in range(2, order):
            tm.append(2.0 * center * tm[-1] - tm[-2])
        s_ref[...] = jnp.zeros_like(s_ref)
        for j in range(order):
            s_ref[j : j + 1, full] = tm[j]
        a_ref[:, full] = jnp.dot(
            series_ref[...], s_ref[:, full], precision=lax.Precision.HIGHEST, preferred_element_type=F32
        )
        first = slab * GS + start
        acc_ref[...] = jnp.zeros_like(acc_ref)

        def chunk(i, carry):
            at = pl.multiple_of(i * 2 * cols, 2 * cols)
            span = pl.ds(at, 2 * cols)
            u_ref[:, full] = dot3(eh[span, :], el[span, :], wh[:, full], wl[:, full])
            sn, cs = sincos(col_ref[i, :, 0:1] + first * col_ref[i, :, 128:129])
            for b0 in range(0, nblk, 8):
                for l0 in range(0, width, 128):
                    ll = slice(l0, l0 + 128)
                    uc = [u_ref[k * nblk + b0 : k * nblk + b0 + 8, ll] for k in range(order)]
                    us = [u_ref[cols + k * nblk + b0 : cols + k * nblk + b0 + 8, ll] for k in range(order)]
                    s8 = sn[b0 : b0 + 8, ll]
                    c8 = cs[b0 : b0 + 8, ll]
                    for j in range(order):
                        vc = vs = None
                        for k in range(j + 1):
                            a = a_ref[j * order + k : j * order + k + 1, ll]
                            vc = a * uc[k] if vc is None else vc + a * uc[k]
                            vs = a * us[k] if vs is None else vs + a * us[k]
                        at_j = j * nblk + b0
                        vr[at_j : at_j + 8, ll] = c8 * vc - s8 * vs
                        vi[at_j : at_j + 8, ll] = s8 * vc + c8 * vs
            both = pp[i]
            ph, pl_ = both[:rows], both[rows:]
            rh, rl = split(vr[:, full])
            ih, il = split(vi[:, full])
            acc_ref[:, full] += dot3(ph, pl_, rh, rl) + dot3(turned(ph), turned(pl_), ih, il)
            return carry

        lax.fori_loop(0, n, chunk, 0)
        return acc_ref[:, full]

    for g in range(0, count, GROUP):
        gg = slice(g, g + GROUP)
        cell = cell_ref[:, gg]
        start = jnp.clip(cell - (TAPS // 2 - 1), 0, GS - WIN)
        val_ref[:, gg] = piece(GROUP, own_ref[:, gg], cell, off_ref[:, gg], own_ref[:, gg], start, cell >= 0)

    owner = own_ref[...]
    cell = cell_ref[...]
    left = cell < TAPS // 2 - 1
    right = cell + TAPS // 2 >= GS
    side = (left & (owner > 0)) | (right & (owner < n_dev - 1))
    sidef = side.astype(F32)
    upto = (
        lax.broadcasted_iota(jnp.int32, (count, count), 0) <= lax.broadcasted_iota(jnp.int32, (count, count), 1)
    ).astype(F32).astype(BF16)
    rank = jnp.dot(sidef.astype(BF16), upto, preferred_element_type=F32).astype(jnp.int32) - 1
    table = jnp.concatenate(
        [owner.astype(F32), cell.astype(F32), off_ref[...].astype(F32), sidef, jnp.zeros((4, count), F32)], 0
    )
    groups = (jnp.sum(side.astype(jnp.int32)) + SIDE - 1) // SIDE

    def side_group(g, carry):
        slot = lax.broadcasted_iota(jnp.int32, (SIDE, count), 0) + g * SIDE
        chosen = ((slot == rank) & side).astype(F32)
        packed = lax.dot_general(
            table, chosen, (((1,), (1,)), ((), ())), precision=lax.Precision.HIGHEST, preferred_element_type=F32
        ).astype(jnp.int32)
        p_owner, p_cell, p_off, p_ok = (packed[a : a + 1] for a in range(4))
        p_left = p_cell < TAPS // 2 - 1
        slab = jnp.where(p_left, p_owner - 1, p_owner + 1)
        out = piece(SIDE, p_owner, p_cell, p_off, slab, jnp.where(p_left, GS - WIN, 0), p_ok > 0)
        hi, lo = split(out)
        put = chosen.astype(BF16)
        val_ref[...] += jnp.dot(hi, put, preferred_element_type=F32) + jnp.dot(lo, put, preferred_element_type=F32)
        return carry

    lax.fori_loop(0, groups, side_group, 0)
    store.wait()


def body(n_slab, n, panels, block_phase, target_owner, target_cell, target_offset):
    n_dev = n_slab * n
    channels = panels.shape[0]
    nblk = block_phase.shape[1]
    order = panels.shape[1] // nblk
    cols = order * nblk
    targets = target_cell.shape[0]
    (mh, ml), series = tables(order, nblk)
    pan, ph = gathered(n, panels, block_phase)
    vmem = pl.BlockSpec(memory_space=pltpu.VMEM)
    hbm = pl.BlockSpec(memory_space=pl.ANY)
    return pl.pallas_call(
        functools.partial(work_kernel, n, n_dev, order, nblk),
        out_shape=(
            jax.ShapeDtypeStruct((channels, GS), F32),
            jax.ShapeDtypeStruct((channels, targets), F32),
        ),
        in_specs=[vmem] * 8 + [hbm] * 2,
        out_specs=(hbm, vmem),
        scratch_shapes=[
            pltpu.VMEM((2, TILES, cols, cols), BF16),
            pltpu.SemaphoreType.DMA((2,)),
            pltpu.SemaphoreType.DMA,
            pltpu.VMEM((n, nblk, 256), jnp.int32),
            pltpu.VMEM((n, 8, cols), jnp.int32),
            pltpu.VMEM((n * 2 * cols, TILE), BF16),
            pltpu.VMEM((n * 2 * cols, TILE), BF16),
            pltpu.VMEM((TILES * channels, n * 2 * cols), BF16),
            pltpu.VMEM((TILES * channels, n * 2 * cols), BF16),
            pltpu.VMEM((channels, GS), F32),
            pltpu.VMEM((n * 2 * cols, WIN), BF16),
            pltpu.VMEM((n * 2 * cols, WIN), BF16),
            pltpu.VMEM((WIN, GROUP), BF16),
            pltpu.VMEM((WIN, GROUP), BF16),
            pltpu.VMEM((order * order, GROUP), F32),
            pltpu.VMEM((2 * cols, GROUP), F32),
            pltpu.VMEM((cols, GROUP), F32),
            pltpu.VMEM((cols, GROUP), F32),
            pltpu.VMEM((128, GROUP), F32),
            pltpu.VMEM((n, 2 * channels, cols), BF16),
            pltpu.VMEM((channels, GROUP), F32),
        ],
        compiler_params=pltpu.CompilerParams(vmem_limit_bytes=56 << 20),
    )(
        pan,
        ph,
        local_cheb(TILE, order),
        local_cheb(WIN, order),
        series,
        target_owner.reshape(1, targets),
        target_cell.reshape(1, targets),
        target_offset.reshape(1, targets),
        mh,
        ml,
    )


def solution(mesh):
    placed = (
        P(None, "term"),
        P(None, "term"),
        P(("slab", "term"), None),
        P(("slab", "term")),
        P(("slab", "term")),
    )
    return jax.shard_map(
        functools.partial(body, mesh.shape["slab"], mesh.shape["term"]),
        mesh=mesh,
        in_specs=placed,
        out_specs=(P(None, ("slab", "term")), P(None, ("slab", "term"))),
        check_vma=False,
    )
```

time: 64.6 us -> 36.2 us (0.56)
  Pallas kernels: 51 us -> 35.4 us
  local copies, waits for them, and re-layouts: 11.7 us -> 0 us
  other arithmetic: 0.68 us -> 0 us
    pallas_call x2 -> x1, Pallas kernels: 38.7 us -> 25 us  [body(): pl.pallas_call(functools.partial(work_kernel, n, n_dev, order, nblk), out...]
    unnamed x22 -> x0, local copies, waits for them, and re-layouts: 9.26 us -> none
    pallas_call x1, Pallas kernels: 12.3 us -> 10.3 us  [gathered(): pl.pallas_call(functools.partial(gather_kernel, n), out_shape=(jax.ShapeD...]
    transpose x2 -> x0, local copies, waits for them, and re-layouts: 0.8 us -> none  [the longest x1 0.76 us: body(): tall = jnp.repeat(block_phase.T, cols // 2, axis=1)]
    another operation x2 -> x0, local copies, waits for them, and re-layouts: 0.77 us -> none  [body(): wide = jnp.tile(block_phase, (1, order))]
    reshape x1 -> x0, local copies, waits for them, and re-layouts: 0.71 us -> none  [body(): panels.reshape(channels, nblk, order).swapaxes(1, 2).reshape(channels, cols)]
    concatenate x1 -> x0, other arithmetic: 0.68 us -> none  [body(): ph = jnp.concatenate([wide, jnp.zeros((6, cols), jnp.int32), tall], 0)]
where the time goes in v2:
time: 36.2 us; the launch traced here: 36 us
  Pallas kernels  35.4 us (98%)
  between operations  0.64 us (2%)
    pallas_call x1, Pallas kernels, body(): pl.pallas_call(functools.partial(work_kernel, n, n_dev, order, nblk), out...  25 us
    pallas_call x1, Pallas kernels, gathered(): pl.pallas_call(functools.partial(gather_kernel, n), out_shape=(jax.ShapeD...  10.3 us

profile of v2, /device:TPU:0, one launch (start us, length us, event | category | flops | bytes accessed | tf_op | source)
XLA Modules:
  0.0 36.0 jit_solution(1504756510401568653)
XLA Ops:
  0.6 10.3 %shard_map.113 = (f32[4,64,256]{2,1,0:T(8,128)}, s32[4,2,16]{2,1,0:T(2,128)}) custom-call(f32[64,256]{1,0:T(8,128)} %pan_ref.1, s32[2,16]{1,0:T(2,128)} %ph_ref.1), custom_call_target="tpu_custom_call" | custom-call | tf_op jit(solution)/shard_map/pallas_call | solution.py:155
  11.0 25.0 %shard_map.114 = (f32[64,6144]{1,0:T(8,128)}, f32[64,512]{1,0:T(8,128)}) custom-call(f32[4,64,256]{2,1,0:T(8,128)} %get-tuple-element.4.pan_ref, s32[4,2,16]{2,1,0:T(2,128)} %get-tuple-element.5.ph_ref, f32[16,1024]{1,0:T(8,128)} %constant.10.clone.cheb_ref, f32[16,256]{1,0:T(8,128)} %constant.11.clone.wcheb_ref, f32[256,128]{1,0:T(8,128)} %constant.12.clone.series_ref, ...), custom_call_target="tpu_custom_call" | custom-call | tf_op jit(solution)/shard_map/pallas_call | solution.py:371
